TPU v7x, 32 devices: a whole 2x2x4 slice. The times are simulated.
32 devices in a mesh: dp: 4 (over z), blk: 4 (over x, core), uly: 2 (over y).
Axes of the slice: x: 2, y: 2, z: 4, core: 2. Of those that a mesh axis runs over, the one named last changes fastest.
Arguments:
- query_act: bfloat16 [4, 512, 2048], P('dp', ('blk', 'uly')), may hold values from -8.7 to 8.7
- key_act: bfloat16 [4, 512, 512], P('dp', ('blk', 'uly')), may hold values from -8.7 to 8.7
- value_act: bfloat16 [4, 512, 512], P('dp', ('blk', 'uly')), may hold values from -6 to 6
- out_grad: bfloat16 [4, 512, 2048], P('dp', ('blk', 'uly')), may hold values from -4 to 4
- layer_input: bfloat16 [4, 512, 3072], P('dp', 'blk'), may hold values from -5 to 5
- segments: int32 [4, 512], P('dp'), may hold values from 0 to 3, never falling along the last dimension, each value on 1 to 256 neighbouring positions
- allow_table: int32 [4, 4, 4], P('dp', 'blk'), may hold values from 0 to 1, as said below
Outputs:
- query_grad: bfloat16 [4, 512, 2048], P('dp', 'blk', 'uly')
- key_grad: bfloat16 [4, 512, 512], P('dp', 'blk', 'uly')
- value_grad: bfloat16 [4, 512, 512], P('dp', 'blk', 'uly')
- weight_grad: float32 [3072, 512], P(('dp', 'blk'), 'uly')
Inputs may be any that keep to these rules, and one draw needn't show every extreme that they name: allow_table[d, i, 0] is 1: every query block takes keys from its own block.
All inputs are finite; a program needn't handle non-finite values.
Results may differ from a plain program's by a relative error of at most 0.0096.
Values may be sent and summed in bfloat16 or wider, within the bound.
A program may use at most 64 MiB of HBM per device.

v0:
```python
import functools

import jax
import jax.numpy as jnp
from jax import lax
from jax.experimental import pallas as pl
from jax.experimental.pallas import tpu as pltpu
from jax.sharding import PartitionSpec as P

DH = 128
GROUP = 4
MESH = pl.DeviceIdType.MESH
NEG = -1e30
CUT = None


def dot(a, b, ca, cb):
    return lax.dot_general(a, b, (((ca,), (cb,)), ((), ())), preferred_element_type=jnp.float32)


class Send:
    def __init__(self, cp):
        self.cp, self.started, self.landed = cp, False, False

    def start(self):
        self.started = True
        self.cp.start()

    def wait_recv(self):
        if self.started and not self.landed:
            self.landed = True
            self.cp.wait_recv()

    def finish(self):
        if self.started:
            self.wait_recv()
            self.cp.wait_send()


def kernel(cut, *args):
    sends = []
    for name in stages(sends, *args):
        if name == cut:
            break
    for cp in sends:
        cp.finish()


def stages(sends, nd, nb, nh, rows, cols, weights, *refs):
    if weights:
        (q, k, v, g, seg_in, allow_in, x_in, q_out, k_out, v_out, w_out,
         qb, gb, kv, bias, pv, pk, rv, rk, ownv, ownk, seg, allow, x, xt, xall, vg, ws, wr,
         ls, ys, yr, fs, fr, ps, pr, xs, xr, zs, zr, cs, cr, hs, hr) = refs
    else:
        (q, k, v, g, seg_in, allow_in, q_out, k_out, v_out,
         qb, gb, kv, bias, pv, pk, rv, rk, ownv, ownk, seg, allow,
         ls, ys, yr, fs, fr, ps, pr) = refs
    d, b, u = lax.axis_index("dp"), lax.axis_index("blk"), lax.axis_index("uly")
    other = 1 - u
    half = rows // 2
    core, side = lax.rem(b, 2), b // 2
    twin = {"blk": side * 2 + 1 - core}
    across = {"blk": (1 - side) * 2 + core}
    slot = 2 * d + core
    scale = DH ** (-0.5)
    width = GROUP * DH

    mine = pl.ds(pl.multiple_of(u * half, half), half)
    window_mine = pl.ds(pl.multiple_of(b * rows + u * half, half), half)
    block_mine = pl.ds(pl.multiple_of(b * rows, rows), rows)
    to_y = {"uly": other}

    def head_cols(who, c, w):
        return pl.ds(pl.multiple_of((who * nh + c) * w, w), w)

    barrier = pltpu.get_barrier_semaphore()
    count = 1
    pl.semaphore_signal(barrier, inc=1, device_id={"uly": other}, device_id_type=MESH)
    for r in range(1, nb):
        pl.semaphore_signal(
            barrier, inc=1, device_id={"blk": lax.rem(b + r, nb)}, device_id_type=MESH)
        count += 1
    if weights:
        for r in range(1, nd):
            for tc in (core, 1 - core):
                pl.semaphore_signal(
                    barrier, inc=1,
                    device_id={"dp": lax.rem(d + r, nd), "blk": side * 2 + tc},
                    device_id_type=MESH)
                count += 1

    local = []

    def fetch(src, dst):
        cp = pltpu.make_async_copy(src, dst, ls.at[len(local)])
        cp.start()
        local.append(cp)

    if weights:
        fetch(x_in, x)
    fetch(seg_in, seg)
    fetch(allow_in, allow)
    for c in range(nh):
        fetch(k.at[:, head_cols(u, c, DH)], kv.at[c, 0, window_mine])
        fetch(v.at[:, head_cols(u, c, DH)], kv.at[c, 1, window_mine])
        fetch(q.at[:, head_cols(u, c, width)], qb.at[c, mine])
        fetch(g.at[:, head_cols(u, c, width)], gb.at[c, mine])
    if weights:
        local.pop(0).wait()
        for t in range(xt.shape[0] // 128):
            xt[t * 128:(t + 1) * 128, :] = x[:, t * 128:(t + 1) * 128].T
    pl.semaphore_wait(barrier, count)
    yield "barrier"

    def copy(src, dst, s, r, to):
        cp = Send(pltpu.make_async_remote_copy(
            src_ref=src, dst_ref=dst, send_sem=s, recv_sem=r, device_id=to, device_id_type=MESH))
        sends.append(cp)
        return cp

    ky, qy = [], []
    for c in range(nh):
        for n, src in enumerate((k, v)):
            ky.append(copy(src.at[:, head_cols(other, c, DH)], kv.at[c, n, window_mine],
                           ys.at[c, n], yr.at[c, n], to_y))
    for c in range(nh):
        for n, (src, dst) in enumerate(((q, qb), (g, gb))):
            qy.append(copy(src.at[:, head_cols(other, c, width)], dst.at[c, mine],
                           ys.at[c, 2 + n], yr.at[c, 2 + n], to_y))
    for cp in ky + qy:
        cp.start()
    def my_rows(who):
        return pl.ds(pl.multiple_of(who * rows, rows), rows)

    def column_rows(td, part, tc):
        return pl.ds(pl.multiple_of((td * nb + 2 * part + tc) * cols, 16), cols)

    xcopies = []
    if weights:
        for r in range(nd):
            td = lax.rem(d + r, nd)
            for n, tc in enumerate((core, 1 - core)):
                if r == 0 and n == 0:
                    continue
                cp = copy(xt.at[column_rows(td, u, tc)],
                          xall.at[u, :, my_rows(slot)],
                          xs.at[r, n, 0], xr.at[r, n, 0],
                          {"dp": td, "blk": side * 2 + tc})
                cp.start()
                xcopies.append(cp)
        xall[u, :, my_rows(slot)] = xt[column_rows(d, u, core), :]

    for cp in local:
        cp.wait()
    yield 'xt'
    fwd = [[] for _ in range(nh)]
    for c in range(nh):
        ky[2 * c].wait_recv()
        ky[2 * c + 1].wait_recv()
        for r in range(1, nb):
            cp = copy(kv.at[c, :, block_mine], kv.at[c, :, block_mine],
                      fs.at[c, r], fr.at[c, r], {"blk": lax.rem(b + r, nb)})
            cp.start()
            fwd[c].append(cp)

    yield 'fwd'
    i0 = lax.broadcasted_iota(jnp.int32, (rows, rows), 0)
    i1 = lax.broadcasted_iota(jnp.int32, (rows, rows), 1)
    seg_p = seg[:, pl.ds(pl.multiple_of(b * rows, rows), rows)]
    lane = lax.broadcasted_iota(jnp.int32, (1, nb), 1)
    table = allow[...]
    for j in range(nb):
        seg_j = jnp.broadcast_to(seg[:, j * rows:(j + 1) * rows], (rows, rows))
        seg_t = jnp.sum(jnp.where(i0 == i1, seg_j, 0), axis=1, keepdims=True)
        step = lax.rem(b - j + nb, nb)
        ok = jnp.sum(jnp.where(lane == step, table, 0), axis=1, keepdims=True)
        seen = (j * rows + i0 <= b * rows + i1) & (seg_t == seg_p) & (ok == 1)
        bias[j * rows:(j + 1) * rows, :] = jnp.where(seen, 0.0, NEG)

    yield 'mask'

    def four(ref, c):
        return jnp.concatenate(
            [ref[c, :, h * DH:(h + 1) * DH] for h in range(GROUP)], axis=0)

    parts_v, parts_k, far, partial = [], [], [], []
    near = [[] for _ in range(nh)]

    def send_parts(c, n, out, stage, land, own, keep):
        for j in range(nb):
            stage[c, j] = out[j * rows:(j + 1) * rows].astype(jnp.bfloat16)
        own[c] = stage[c, b].astype(jnp.float32)
        copies = []
        for r in range(1, nb):
            to = lax.rem(b + r, nb)
            cp = copy(stage.at[c, to], land.at[c, r], ps.at[n, c, r], pr.at[n, c, r],
                      {"blk": to})
            cp.start()
            copies.append(cp)
        keep.append(copies)

    def total(c, copies, land, own):
        for cp in copies[c]:
            cp.wait_recv()
        acc = own[c]
        for r in range(1, nb):
            acc = acc + land[c, r].astype(jnp.float32)
        return acc.astype(jnp.bfloat16)

    def part_one(c):
        for cp in fwd[c]:
            cp.wait_recv()
        qy[2 * c].wait_recv()
        qy[2 * c + 1].wait_recv()
        scores = dot(kv[c, 0], four(qb, c), 1, 1) * scale
        hidden = bias[...]
        scores = scores + jnp.concatenate([hidden] * GROUP, axis=1)
        peak = jnp.max(scores, axis=0, keepdims=True)
        e = jnp.exp(scores - peak)
        probs = e * (1.0 / jnp.sum(e, axis=0, keepdims=True))
        low = probs.astype(jnp.bfloat16)
        send_parts(c, 0, dot(low, four(gb, c), 1, 0), pv, rv, ownv, parts_v)
        return probs, low

    def part_two(c, probs, low):
        grad = dot(kv[c, 1], four(gb, c), 1, 1)
        delta = jnp.sum(low.astype(jnp.float32) * grad, axis=0, keepdims=True)
        ds = (probs * (grad - delta)).astype(jnp.bfloat16)
        send_parts(c, 1, dot(ds, four(qb, c), 1, 0) * scale, pk, rk, ownk, parts_k)
        return ds

    def part_three(c, ds):
        dq = dot(kv[c, 0], ds, 0, 0) * scale
        for h in range(GROUP):
            at = c * width + h * DH
            q_out[:, at:at + DH] = dq[:, h * DH:(h + 1) * DH].T.astype(jnp.bfloat16)

    def to_twin(c, n, who):
        cp = copy(vg.at[c, my_rows(who)], vg.at[c, my_rows(who)], cs.at[c, n], cr.at[c, n], twin)
        cp.start()
        near[c].append(cp)

    def finish_v(c):
        low = total(c, parts_v, rv, ownv)
        v_out[:, c * DH:(c + 1) * DH] = low
        if weights:
            vg[c, my_rows(slot), :] = low
            for r in range(1, nd):
                cp = copy(vg.at[c, my_rows(slot)], vg.at[c, my_rows(slot)],
                          zs.at[c, r], zr.at[c, r], {"dp": lax.rem(d + r, nd)})
                cp.start()
                far.append(cp)
            to_twin(c, 0, slot)

    def forward(c):
        for r in range(1, nd):
            far[c * (nd - 1) + r - 1].wait_recv()
            to_twin(c, r, 2 * lax.rem(d - r + nd, nd) + core)

    def product(c):
        for cp in near[c]:
            cp.wait_recv()
        ws[c] = dot(xall[1 - side], vg[c], 1, 0).astype(jnp.bfloat16)
        cp = copy(ws.at[c], wr.at[c], hs.at[c], hr.at[c], across)
        cp.start()
        partial.append(cp)
        w_out[:, c * DH:(c + 1) * DH] = dot(xall[side], vg[c], 1, 0)

    state = part_one(0)
    yield 'one0'
    grads = [part_two(0, *state)]
    if weights:
        for cp in xcopies:
            cp.wait_recv()
        shared = copy(xall.at[u], xall.at[u], xs.at[0, 0, 1], xr.at[0, 0, 1], to_y)
        shared.start()
    yield 'two0'
    for c in range(1, nh):
        state = part_one(c)
        yield 'one1'
        finish_v(c - 1)
        grads.append(part_two(c, *state))
        yield 'two1'
    finish_v(nh - 1)
    yield 'finish1'
    for c in range(nh):
        part_three(c, grads[c])
    if weights:
        for c in range(nh - 1):
            forward(c)
    yield 'forward0'
    if weights:
        shared.wait_recv()
        for c in range(nh - 1):
            product(c)
    yield 'product0'
    for c in range(nh):
        k_out[:, c * DH:(c + 1) * DH] = total(c, parts_k, rk, ownk)
    yield 'kout'
    if weights:
        forward(nh - 1)
        yield 'forward1'
        product(nh - 1)
        for c in range(nh):
            partial[c].wait_recv()
            w_out[:, c * DH:(c + 1) * DH] += wr[c].astype(jnp.float32)


def emit(*refs):
    n = len(refs) // 2
    copies = [pltpu.make_async_copy(refs[t], refs[n + t], refs[-1].at[t]) for t in range(n)]
    for cp in copies:
        cp.start()
    for cp in copies:
        cp.wait()


def shards(query_act, key_act, value_act, out_grad, layer_input, segments, allow_table):
    nd, nb, nu = lax.axis_size("dp"), lax.axis_size("blk"), lax.axis_size("uly")
    half, qw = query_act.shape[1:]
    rows = half * nu
    kw = key_act.shape[2] // nu
    qw = qw // nu
    nh = kw // DH
    window = rows * nb
    din = layer_input.shape[2]
    cols = din // (nd * nb)
    weights = cols % 16 == 0 and nb == 4 and nd <= 8 and nu == 2
    bf, f32, sem = jnp.bfloat16, jnp.float32, pltpu.SemaphoreType.DMA
    vm = pltpu.VMEM
    scratch = [
        vm((nh, rows, GROUP * DH), bf), vm((nh, rows, GROUP * DH), bf),
        vm((nh, 2, window, DH), bf), vm((window, rows), f32),
        vm((nh, nb, rows, DH), bf), vm((nh, nb, rows, DH), bf),
        vm((nh, nb, rows, DH), bf), vm((nh, nb, rows, DH), bf),
        vm((nh, rows, DH), f32), vm((nh, rows, DH), f32),
        vm(segments.shape, jnp.int32), vm(allow_table.shape[1:], jnp.int32),
    ]
    sems = [sem((4 * nh + 3,)), sem((nh, 4)), sem((nh, 4)), sem((nh, nb)), sem((nh, nb)),
            sem((2, nh, nb)), sem((2, nh, nb))]
    outs = [jax.ShapeDtypeStruct((rows, qw), bf), jax.ShapeDtypeStruct((rows, kw), bf),
            jax.ShapeDtypeStruct((rows, kw), bf)]
    args = [query_act[0], key_act[0], value_act[0], out_grad[0], segments, allow_table[0]]
    if weights:
        args.append(layer_input[0])
        outs.append(jax.ShapeDtypeStruct((cols, kw), f32))
        scratch += [vm((rows, din), bf), vm((din, rows), bf), vm((2, cols, nd * 2 * rows), bf),
                    vm((nh, nd * 2 * rows, DH), bf), vm((nh, cols, DH), bf),
                    vm((nh, cols, DH), bf)]
        sems += [sem((nd, 2, 2)), sem((nd, 2, 2)), sem((nh, nd)), sem((nh, nd)),
                 sem((nh, nd)), sem((nh, nd)), sem((nh,)), sem((nh,))]
    spec = pl.BlockSpec(memory_space=pltpu.VMEM)
    res = pl.pallas_call(
        functools.partial(kernel, CUT, nd, nb, nh, rows, cols, weights),
        out_shape=outs,
        in_specs=[pl.BlockSpec(memory_space=pltpu.HBM)] * len(args),
        out_specs=[spec] * len(outs),
        scratch_shapes=scratch + sems,
        compiler_params=pltpu.CompilerParams(
            collective_id=0, has_side_effects=True, vmem_limit_bytes=52_000_000),
    )(*[pltpu.with_memory_space_constraint(a, pltpu.HBM) for a in args])
    res = pl.pallas_call(
        emit,
        out_shape=outs,
        in_specs=[spec] * len(outs),
        out_specs=[pl.BlockSpec(memory_space=pltpu.HBM)] * len(outs),
        scratch_shapes=[sem((len(outs),))],
        compiler_params=pltpu.CompilerParams(vmem_limit_bytes=2 * 1024 * 1024),
    )(*res)
    if weights:
        weight_out = res[3]
    else:
        weight_out = lax.psum_scatter(
            dot(layer_input[0], res[2], 0, 0), ("dp", "blk"), scatter_dimension=0, tiled=True)
    return (res[0][None], res[1][None], res[2][None], weight_out)


def solution(mesh):
    return jax.shard_map(
        shards,
        mesh=mesh,
        in_specs=(
            P("dp", ("blk", "uly"), None),
            P("dp", ("blk", "uly"), None),
            P("dp", ("blk", "uly"), None),
            P("dp", ("blk", "uly"), None),
            P("dp", "blk", None),
            P("dp", None),
            P("dp", "blk", None),
        ),
        out_specs=(
            P("dp", "blk", "uly"),
            P("dp", "blk", "uly"),
            P("dp", "blk", "uly"),
            P(("dp", "blk"), "uly"),
        ),
        check_vma=False,
    )
```

profile of v0, /device:TPU:0, one launch (start us, length us, event | category | flops | bytes accessed | tf_op | source)
XLA Modules:
  0.0 32.9 jit_solution(4861931549123924658)
XLA Ops:
  0.6 31.4 %shard_map.102 = (bf16[128,1024]{1,0:T(8,128)(2,1)S(1)}, bf16[128,256]{1,0:T(8,128)(2,1)S(1)}, bf16[128,256]{1,0:T(8,128)(2,1)S(1)}, f32[192,256]{1,0:T(8,128)S(1)}) custom-call(bf16[64,2048]{1,0:T(8,128)(2,1)} %bitcast.10, bf16[64,512]{1,0:T(8,128)(2,1)} %bitcast.12, bf16[64,512]{1,0:T(8,128)(2,1)} %bitcast.13, bf16[64,2048]{1,0:T(8,128)(2,1)} %bitcast.11, ...), custom_call_target="tpu_custom_call" | custom-call | tf_op jit(solution)/shard_map/pallas_call | solution.py:353
  32.1 0.8 %shard_map.103 = (bf16[128,1024]{1,0:T(8,128)(2,1)}, bf16[128,256]{1,0:T(8,128)(2,1)}, bf16[128,256]{1,0:T(8,128)(2,1)}, f32[192,256]{1,0:T(8,128)}) custom-call(bf16[128,1024]{1,0:T(8,128)(2,1)S(1)} %get-tuple-element.12.refs_0_, bf16[128,256]{1,0:T(8,128)(2,1)S(1)} %get-tuple-element.13.refs_1_, bf16[128,256]{1,0:T(8,128)(2,1)S(1)} %get-tuple-element.14.refs_2_, ...), custom_call_target="tpu_custom_call" | custom-call | tf_op jit(solution)/shard_map/pallas_call | solution.py:362
where the time goes:
time: 33 us; the launch traced here: 32.9 us
  Pallas kernels  32.3 us (98%)
  between operations  0.64 us (2%)
    pallas_call x1, Pallas kernels, shards(): pl.pallas_call(functools.partial(kernel, CUT, nd, nb, nh, rows, cols, wei...  31.4 us
    pallas_call x1, Pallas kernels, shards(): pl.pallas_call(emit, out_shape=outs, in_specs=[spec] * len(outs), out_spe...  0.84 us

commit v1 on v0

--- a/solution.py
+++ b/solution.py
@@ -18,23 +18,31 @@
     return lax.dot_general(a, b, (((ca,), (cb,)), ((), ())), preferred_element_type=jnp.float32)
 
 
+def guarded(cond, run):
+    if cond is None:
+        run()
+    else:
+        pl.when(cond)(run)
+
+
 class Send:
-    def __init__(self, cp):
-        self.cp, self.started, self.landed = cp, False, False
+    def __init__(self, cp, goes, comes):
+        self.cp, self.goes, self.comes = cp, goes, comes
+        self.started, self.landed = False, False
 
     def start(self):
         self.started = True
-        self.cp.start()
+        guarded(self.goes, self.cp.start)
 
     def wait_recv(self):
         if self.started and not self.landed:
             self.landed = True
-            self.cp.wait_recv()
+            guarded(self.comes, self.cp.wait_recv)
 
     def finish(self):
         if self.started:
             self.wait_recv()
-            self.cp.wait_send()
+            guarded(self.goes, self.cp.wait_send)
 
 
 def kernel(cut, *args):
@@ -50,7 +58,7 @@
     if weights:
         (q, k, v, g, seg_in, allow_in, x_in, q_out, k_out, v_out, w_out,
          qb, gb, kv, bias, pv, pk, rv, rk, ownv, ownk, seg, allow, x, xt, xall, vg, ws, wr,
-         ls, ys, yr, fs, fr, ps, pr, xs, xr, zs, zr, cs, cr, hs, hr) = refs
+         ls, ys, yr, fs, fr, ps, pr, xs, xr, zs, zr, cs, cr, hs, hr, hx, hy) = refs
     else:
         (q, k, v, g, seg_in, allow_in, q_out, k_out, v_out,
          qb, gb, kv, bias, pv, pk, rv, rk, ownv, ownk, seg, allow,
@@ -67,7 +75,7 @@
 
     mine = pl.ds(pl.multiple_of(u * half, half), half)
     window_mine = pl.ds(pl.multiple_of(b * rows + u * half, half), half)
-    block_mine = pl.ds(pl.multiple_of(b * rows, rows), rows)
+    window_other = pl.ds(pl.multiple_of(b * rows + other * half, half), half)
     to_y = {"uly": other}
 
     def head_cols(who, c, w):
@@ -96,8 +104,6 @@
         cp.start()
         local.append(cp)
 
-    if weights:
-        fetch(x_in, x)
     fetch(seg_in, seg)
     fetch(allow_in, allow)
     for c in range(nh):
@@ -106,15 +112,13 @@
         fetch(q.at[:, head_cols(u, c, width)], qb.at[c, mine])
         fetch(g.at[:, head_cols(u, c, width)], gb.at[c, mine])
     if weights:
-        local.pop(0).wait()
-        for t in range(xt.shape[0] // 128):
-            xt[t * 128:(t + 1) * 128, :] = x[:, t * 128:(t + 1) * 128].T
+        fetch(x_in, x)
     pl.semaphore_wait(barrier, count)
-    yield "barrier"
-
-    def copy(src, dst, s, r, to):
+
+    def copy(src, dst, s, r, to, goes=None, comes=None):
         cp = Send(pltpu.make_async_remote_copy(
-            src_ref=src, dst_ref=dst, send_sem=s, recv_sem=r, device_id=to, device_id_type=MESH))
+            src_ref=src, dst_ref=dst, send_sem=s, recv_sem=r, device_id=to,
+            device_id_type=MESH), goes, comes)
         sends.append(cp)
         return cp
 
@@ -127,42 +131,71 @@
         for n, (src, dst) in enumerate(((q, qb), (g, gb))):
             qy.append(copy(src.at[:, head_cols(other, c, width)], dst.at[c, mine],
                            ys.at[c, 2 + n], yr.at[c, 2 + n], to_y))
-    for cp in ky + qy:
-        cp.start()
+    for c in range(nh):
+        for cp in (ky[2 * c], ky[2 * c + 1], qy[2 * c], qy[2 * c + 1]):
+            cp.start()
+
+    fwd = [[] for _ in range(nh)]
+    for c in range(nh):
+        for r in range(1, nb):
+            for n, src in enumerate((k, v)):
+                cp = copy(src.at[:, head_cols(u, c, DH)], kv.at[c, n, window_mine],
+                          fs.at[c, r, n], fr.at[c, r, n], {"blk": lax.rem(b + r, nb)},
+                          b + r < nb, b >= r)
+                cp.start()
+                fwd[c].append(cp)
     def my_rows(who):
         return pl.ds(pl.multiple_of(who * rows, rows), rows)
 
     def column_rows(td, part, tc):
         return pl.ds(pl.multiple_of((td * nb + 2 * part + tc) * cols, 16), cols)
 
-    xcopies = []
-    if weights:
-        for r in range(nd):
-            td = lax.rem(d + r, nd)
-            for n, tc in enumerate((core, 1 - core)):
-                if r == 0 and n == 0:
-                    continue
-                cp = copy(xt.at[column_rows(td, u, tc)],
-                          xall.at[u, :, my_rows(slot)],
-                          xs.at[r, n, 0], xr.at[r, n, 0],
-                          {"dp": td, "blk": side * 2 + tc})
-                cp.start()
-                xcopies.append(cp)
-        xall[u, :, my_rows(slot)] = xt[column_rows(d, u, core), :]
-
-    for cp in local:
-        cp.wait()
-    yield 'xt'
-    fwd = [[] for _ in range(nh)]
-    for c in range(nh):
+    def forward_kv(c):
         ky[2 * c].wait_recv()
         ky[2 * c + 1].wait_recv()
         for r in range(1, nb):
-            cp = copy(kv.at[c, :, block_mine], kv.at[c, :, block_mine],
-                      fs.at[c, r], fr.at[c, r], {"blk": lax.rem(b + r, nb)})
+            cp = copy(kv.at[c, :, window_other], kv.at[c, :, window_other],
+                      fs.at[c, r, 2], fr.at[c, r, 2], {"blk": lax.rem(b + r, nb)},
+                      b + r < nb, b >= r)
             cp.start()
             fwd[c].append(cp)
 
+    for cp in local:
+        cp.wait()
+    for j in range(1, nb):
+        @pl.when(j > b)
+        def _():
+            kv[:, :, j * rows:(j + 1) * rows, :] = jnp.zeros((nh, 2, rows, DH), jnp.bfloat16)
+
+        @pl.when(b >= j)
+        def _():
+            rv[:, j] = jnp.zeros((nh, rows, DH), jnp.bfloat16)
+            rk[:, j] = jnp.zeros((nh, rows, DH), jnp.bfloat16)
+    yield 'barrier'
+    forward_kv(0)
+
+    xtwin, xfar = [], [[] for _ in range(nd)]
+    if weights:
+        for t in range(xt.shape[0] // 128):
+            xt[t * 128:(t + 1) * 128, :] = x[:, t * 128:(t + 1) * 128].T
+        for r in range(1, nd):
+            td = lax.rem(d + r, nd)
+            for n, tc in enumerate((core, 1 - core)):
+                cp = copy(xt.at[column_rows(td, u, tc)],
+                          xall.at[u, :, my_rows(slot)],
+                          xs.at[r, n], xr.at[r, n],
+                          {"dp": td, "blk": side * 2 + tc})
+                cp.start()
+                xfar[r].append(cp)
+        for part in range(2):
+            cp = copy(xt.at[column_rows(d, part, 1 - core)], xall.at[part, :, my_rows(slot)],
+                      xs.at[0, part], xr.at[0, part], twin)
+            cp.start()
+            xtwin.append(cp)
+            xall[part, :, my_rows(slot)] = xt[column_rows(d, part, core), :]
+    yield 'xt'
+    for c in range(1, nh):
+        forward_kv(c)
     yield 'fwd'
     i0 = lax.broadcasted_iota(jnp.int32, (rows, rows), 0)
     i1 = lax.broadcasted_iota(jnp.int32, (rows, rows), 1)
@@ -194,7 +227,7 @@
         for r in range(1, nb):
             to = lax.rem(b + r, nb)
             cp = copy(stage.at[c, to], land.at[c, r], ps.at[n, c, r], pr.at[n, c, r],
-                      {"blk": to})
+                      {"blk": to}, b + r >= nb, b < r)
             cp.start()
             copies.append(cp)
         keep.append(copies)
@@ -266,22 +299,32 @@
         partial.append(cp)
         w_out[:, c * DH:(c + 1) * DH] = dot(xall[side], vg[c], 1, 0)
 
+    shared = []
+
+    def share(r):
+        if weights and r < nd:
+            for cp in xfar[r]:
+                cp.wait_recv()
+            pair = pl.ds(pl.multiple_of(2 * lax.rem(d - r + nd, nd) * rows, 2 * rows), 2 * rows)
+            cp = copy(xall.at[u, :, pair], xall.at[u, :, pair], hx.at[r], hy.at[r], to_y)
+            cp.start()
+            shared.append(cp)
+
     state = part_one(0)
     yield 'one0'
     grads = [part_two(0, *state)]
-    if weights:
-        for cp in xcopies:
-            cp.wait_recv()
-        shared = copy(xall.at[u], xall.at[u], xs.at[0, 0, 1], xr.at[0, 0, 1], to_y)
-        shared.start()
+    share(1)
     yield 'two0'
     for c in range(1, nh):
         state = part_one(c)
         yield 'one1'
         finish_v(c - 1)
+        share(c + 1)
         grads.append(part_two(c, *state))
         yield 'two1'
     finish_v(nh - 1)
+    for r in range(nh + 1, nd):
+        share(r)
     yield 'finish1'
     for c in range(nh):
         part_three(c, grads[c])
@@ -290,7 +333,8 @@
             forward(c)
     yield 'forward0'
     if weights:
-        shared.wait_recv()
+        for cp in shared + xtwin:
+            cp.wait_recv()
         for c in range(nh - 1):
             product(c)
     yield 'product0'
@@ -336,7 +380,7 @@
         vm((nh, rows, DH), f32), vm((nh, rows, DH), f32),
         vm(segments.shape, jnp.int32), vm(allow_table.shape[1:], jnp.int32),
     ]
-    sems = [sem((4 * nh + 3,)), sem((nh, 4)), sem((nh, 4)), sem((nh, nb)), sem((nh, nb)),
+    sems = [sem((4 * nh + 3,)), sem((nh, 4)), sem((nh, 4)), sem((nh, nb, 3)), sem((nh, nb, 3)),
             sem((2, nh, nb)), sem((2, nh, nb))]
     outs = [jax.ShapeDtypeStruct((rows, qw), bf), jax.ShapeDtypeStruct((rows, kw), bf),
             jax.ShapeDtypeStruct((rows, kw), bf)]
@@ -347,8 +391,9 @@
         scratch += [vm((rows, din), bf), vm((din, rows), bf), vm((2, cols, nd * 2 * rows), bf),
                     vm((nh, nd * 2 * rows, DH), bf), vm((nh, cols, DH), bf),
                     vm((nh, cols, DH), bf)]
-        sems += [sem((nd, 2, 2)), sem((nd, 2, 2)), sem((nh, nd)), sem((nh, nd)),
-                 sem((nh, nd)), sem((nh, nd)), sem((nh,)), sem((nh,))]
+        sems += [sem((nd, 2)), sem((nd, 2)), sem((nh, nd)), sem((nh, nd)),
+                 sem((nh, nd)), sem((nh, nd)), sem((nh,)), sem((nh,)),
+                 sem((nd,)), sem((nd,))]
     spec = pl.BlockSpec(memory_space=pltpu.VMEM)
     res = pl.pallas_call(
         functools.partial(kernel, CUT, nd, nb, nh, rows, cols, weights),

time: 33 us -> 31.7 us (0.961)
  Pallas kernels: 32.3 us -> 30.9 us
    pallas_call x1, Pallas kernels: 31.4 us -> 30.1 us  [shards(): pl.pallas_call(functools.partial(kernel, CUT, nd, nb, nh, rows, cols, wei...]
where the time goes in v1:
time: 31.7 us; the launch traced here: 31.5 us
  Pallas kernels  30.9 us (97%)
  between operations  0.64 us (2%)
    pallas_call x1, Pallas kernels, shards(): pl.pallas_call(functools.partial(kernel, CUT, nd, nb, nh, rows, cols, wei...  30.1 us
    pallas_call x1, Pallas kernels, shards(): pl.pallas_call(emit, out_shape=outs, in_specs=[spec] * len(outs), out_spe...  0.84 us

profile of v1, /device:TPU:0, one launch (start us, length us, event | category | flops | bytes accessed | tf_op | source)
XLA Modules:
  0.0 31.5 jit_solution(17328606117385755350)
XLA Ops:
  0.6 30.1 %shard_map.102 = (bf16[128,1024]{1,0:T(8,128)(2,1)S(1)}, bf16[128,256]{1,0:T(8,128)(2,1)S(1)}, bf16[128,256]{1,0:T(8,128)(2,1)S(1)}, f32[192,256]{1,0:T(8,128)S(1)}) custom-call(bf16[64,2048]{1,0:T(8,128)(2,1)} %bitcast.10, bf16[64,512]{1,0:T(8,128)(2,1)} %bitcast.12, bf16[64,512]{1,0:T(8,128)(2,1)} %bitcast.13, bf16[64,2048]{1,0:T(8,128)(2,1)} %bitcast.11, ...), custom_call_target="tpu_custom_call" | custom-call | tf_op jit(solution)/shard_map/pallas_call | solution.py:398
  30.7 0.8 %shard_map.103 = (bf16[128,1024]{1,0:T(8,128)(2,1)}, bf16[128,256]{1,0:T(8,128)(2,1)}, bf16[128,256]{1,0:T(8,128)(2,1)}, f32[192,256]{1,0:T(8,128)}) custom-call(bf16[128,1024]{1,0:T(8,128)(2,1)S(1)} %get-tuple-element.12.refs_0_, bf16[128,256]{1,0:T(8,128)(2,1)S(1)} %get-tuple-element.13.refs_1_, bf16[128,256]{1,0:T(8,128)(2,1)S(1)} %get-tuple-element.14.refs_2_, ...), custom_call_target="tpu_custom_call" | custom-call | tf_op jit(solution)/shard_map/pallas_call | solution.py:407

commit v2 on v1

--- a/solution.py
+++ b/solution.py
@@ -160,22 +160,9 @@
             cp.start()
             fwd[c].append(cp)
 
-    for cp in local:
-        cp.wait()
-    for j in range(1, nb):
-        @pl.when(j > b)
-        def _():
-            kv[:, :, j * rows:(j + 1) * rows, :] = jnp.zeros((nh, 2, rows, DH), jnp.bfloat16)
-
-        @pl.when(b >= j)
-        def _():
-            rv[:, j] = jnp.zeros((nh, rows, DH), jnp.bfloat16)
-            rk[:, j] = jnp.zeros((nh, rows, DH), jnp.bfloat16)
-    yield 'barrier'
-    forward_kv(0)
-
     xtwin, xfar = [], [[] for _ in range(nd)]
     if weights:
+        local.pop().wait()
         for t in range(xt.shape[0] // 128):
             xt[t * 128:(t + 1) * 128, :] = x[:, t * 128:(t + 1) * 128].T
         for r in range(1, nd):
@@ -193,6 +180,20 @@
             cp.start()
             xtwin.append(cp)
             xall[part, :, my_rows(slot)] = xt[column_rows(d, part, core), :]
+    for cp in local:
+        cp.wait()
+    for j in range(1, nb):
+        @pl.when(j > b)
+        def _():
+            kv[:, :, j * rows:(j + 1) * rows, :] = jnp.zeros((nh, 2, rows, DH), jnp.bfloat16)
+
+        @pl.when(b >= j)
+        def _():
+            rv[:, j] = jnp.zeros((nh, rows, DH), jnp.bfloat16)
+            rk[:, j] = jnp.zeros((nh, rows, DH), jnp.bfloat16)
+    yield 'barrier'
+    forward_kv(0)
+
     yield 'xt'
     for c in range(1, nh):
         forward_kv(c)
@@ -244,7 +245,6 @@
         for cp in fwd[c]:
             cp.wait_recv()
         qy[2 * c].wait_recv()
-        qy[2 * c + 1].wait_recv()
         scores = dot(kv[c, 0], four(qb, c), 1, 1) * scale
         hidden = bias[...]
         scores = scores + jnp.concatenate([hidden] * GROUP, axis=1)
@@ -252,6 +252,7 @@
         e = jnp.exp(scores - peak)
         probs = e * (1.0 / jnp.sum(e, axis=0, keepdims=True))
         low = probs.astype(jnp.bfloat16)
+        qy[2 * c + 1].wait_recv()
         send_parts(c, 0, dot(low, four(gb, c), 1, 0), pv, rv, ownv, parts_v)
         return probs, low
 

time: 31.7 us -> 30.7 us (0.968)
  Pallas kernels: 30.9 us -> 29.9 us
    pallas_call x1, Pallas kernels: 30.1 us -> 29 us  [shards(): pl.pallas_call(functools.partial(kernel, CUT, nd, nb, nh, rows, cols, wei...]
where the time goes in v2:
time: 30.7 us; the launch traced here: 30.5 us
  Pallas kernels  29.9 us (97%)
  between operations  0.64 us (2%)
    pallas_call x1, Pallas kernels, shards(): pl.pallas_call(functools.partial(kernel, CUT, nd, nb, nh, rows, cols, wei...  29 us
    pallas_call x1, Pallas kernels, shards(): pl.pallas_call(emit, out_shape=outs, in_specs=[spec] * len(outs), out_spe...  0.84 us

profile of v2, /device:TPU:0, one launch (start us, length us, event | category | flops | bytes accessed | tf_op | source)
XLA Modules:
  0.0 30.5 jit_solution(16031594417780317360)
XLA Ops:
  0.6 29.0 %shard_map.102 = (bf16[128,1024]{1,0:T(8,128)(2,1)S(1)}, bf16[128,256]{1,0:T(8,128)(2,1)S(1)}, bf16[128,256]{1,0:T(8,128)(2,1)S(1)}, f32[192,256]{1,0:T(8,128)S(1)}) custom-call(bf16[64,2048]{1,0:T(8,128)(2,1)} %bitcast.10, bf16[64,512]{1,0:T(8,128)(2,1)} %bitcast.12, bf16[64,512]{1,0:T(8,128)(2,1)} %bitcast.13, bf16[64,2048]{1,0:T(8,128)(2,1)} %bitcast.11, ...), custom_call_target="tpu_custom_call" | custom-call | tf_op jit(solution)/shard_map/pallas_call | solution.py:399
  29.7 0.8 %shard_map.103 = (bf16[128,1024]{1,0:T(8,128)(2,1)}, bf16[128,256]{1,0:T(8,128)(2,1)}, bf16[128,256]{1,0:T(8,128)(2,1)}, f32[192,256]{1,0:T(8,128)}) custom-call(bf16[128,1024]{1,0:T(8,128)(2,1)S(1)} %get-tuple-element.12.refs_0_, bf16[128,256]{1,0:T(8,128)(2,1)S(1)} %get-tuple-element.13.refs_1_, bf16[128,256]{1,0:T(8,128)(2,1)S(1)} %get-tuple-element.14.refs_2_, ...), custom_call_target="tpu_custom_call" | custom-call | tf_op jit(solution)/shard_map/pallas_call | solution.py:408
